TPU v7x, 32 devices: a whole 2x2x4 slice. The times are simulated.
32 devices in a mesh: leaf: 2 (over core), row: 4 (over y, x), col: 4 (over z).
Axes of the slice: x: 2, y: 2, z: 4, core: 2. Of those that a mesh axis runs over, the one named last changes fastest.
Arguments:
- sketch_leaf: bfloat16 [16384, 256], P(('leaf', 'row'), 'col'), may hold values from -6 to 6
- sketch_sep: bfloat16 [8192, 256], P(('row', 'col')), may hold values from -6 to 6
- leaf_inverse: bfloat16 [16384, 8192], P(('leaf', 'col'), 'row'), as said below
- coupling: bfloat16 [16384, 2048], P(('leaf', 'col'), 'row'), may hold values from -0.0625 to 0.0625
- sep_inverse: bfloat16 [8192, 8192], P('leaf', ('row', 'col'))
- front_map: int32 [2, 16], replicated, may hold values from 0 to 63, as said below
Outputs:
- sketch_out_leaf: float32 [16384, 256], P(('leaf', 'row'), 'col')
- sketch_out_sep: float32 [8192, 256], P(('row', 'col'))
Inputs may be any that keep to these rules, and one draw needn't show every extreme that they name: `front_map`: row block q of every section's coupling lies in separator blocks q * 4 to q * 4 + 3. leaf_inverse and sep_inverse are inverses of lower triangular factor blocks (in natural order), stored in block-cyclic order.
All inputs are finite; a program needn't handle non-finite values.
Results may differ from a plain program's by a relative error of at most 0.024.
Values may be sent and summed in bfloat16 or wider, within the bound.
No kernel may reach another device: no remote copies, remote signals or barrier semaphores. Data moves between devices by JAX's collectives and lax.ppermute only.
A program may use at most 64 MiB of HBM per device.

v0:
```python
import jax
import jax.numpy as jnp
from jax import lax
from jax.sharding import PartitionSpec as P


def contract_rows(left, right):
    return lax.dot_general(
        left, right, (((0,), (0,)), ((), ())), preferred_element_type=jnp.float32
    )


def shards(sketch_leaf, sketch_sep, leaf_inverse, coupling, sep_inverse, front_map):
    columns = sketch_leaf.shape[1] * lax.axis_size("col")
    q_index = lax.axis_index("row") * lax.axis_size("col") + lax.axis_index("col")
    section = lax.axis_index("leaf")
    partial_value = jnp.dot(
        leaf_inverse,
        lax.all_gather(sketch_leaf, "col", axis=1, tiled=True),
        preferred_element_type=jnp.float32,
    )
    front_z = lax.psum_scatter(partial_value, "row", scatter_dimension=1, tiled=True).astype(
        jnp.bfloat16
    )
    coupled_part = contract_rows(coupling, lax.all_gather(front_z, "row", axis=1, tiled=True))
    coupled = lax.psum_scatter(coupled_part, "col", scatter_dimension=0, tiled=True).astype(
        jnp.bfloat16
    )
    block_rows = coupled.shape[0]
    group = sketch_sep.shape[0] // block_rows
    own_slot = front_map[section, q_index] - q_index * group
    blocks = lax.all_gather(coupled, "leaf", axis=0, tiled=True)
    slots = front_map[:, q_index] - q_index * group
    place = (slots[:, None] == jnp.arange(group, dtype=jnp.int32)[None, :]).astype(jnp.bfloat16)
    stacked = blocks.reshape(slots.shape[0], block_rows, columns)
    total = jnp.einsum("sg,sik->gik", place, stacked, preferred_element_type=jnp.float32).reshape(
        group * block_rows, columns
    )
    sep_rhs = (sketch_sep.astype(jnp.float32) - total).astype(jnp.bfloat16)
    sep_part = jnp.dot(sep_inverse, sep_rhs, preferred_element_type=jnp.float32)
    sep_mid = lax.psum(sep_part.astype(jnp.bfloat16), ("row", "col"))
    sketch_out_sep = lax.psum(
        contract_rows(sep_inverse, sep_mid).astype(jnp.bfloat16), "leaf"
    ).astype(jnp.float32)
    sep_round = sketch_out_sep.astype(jnp.bfloat16)
    pulled = lax.dynamic_slice_in_dim(sep_round, own_slot * block_rows, block_rows, 0)
    back_part = jnp.dot(
        coupling,
        lax.all_gather(pulled, "col", axis=0, tiled=True),
        preferred_element_type=jnp.float32,
    )
    back_slice = lax.psum_scatter(
        back_part.astype(jnp.bfloat16), "row", scatter_dimension=1, tiled=True
    ).astype(jnp.float32)
    leaf_rhs = (front_z.astype(jnp.float32) - back_slice).astype(jnp.bfloat16)
    out_part = contract_rows(leaf_inverse, lax.all_gather(leaf_rhs, "row", axis=1, tiled=True))
    sketch_out_leaf = lax.psum_scatter(
        out_part.astype(jnp.bfloat16), "col", scatter_dimension=1, tiled=True
    ).astype(jnp.float32)
    return (sketch_out_leaf, sketch_out_sep)


def solution(mesh):
    placed = (
        P(("leaf", "row"), "col"),
        P(("row", "col"), None),
        P(("leaf", "col"), "row"),
        P(("leaf", "col"), "row"),
        P("leaf", ("row", "col")),
        P(),
    )
    return jax.shard_map(
        shards,
        mesh=mesh,
        in_specs=placed,
        out_specs=(P(("leaf", "row"), "col"), P(("row", "col"), None)),
        check_vma=False,
    )
```

profile of v0, /device:TPU:0, one launch (start us, length us, event | category | flops | bytes accessed | tf_op | source)
XLA Modules:
  0.0 407.7 jit_solution(16510389504449765819)
XLA Ops:
  7.2 0.0 copy-start
  7.2 0.0 all-gather.4.cloned.1.call-start
  7.2 0.7 all-gather.4.cloned.1.call-update
  7.9 0.0 reduce-scatter.5.cloned.1.call-start
  8.0 32.3 %all-gather.4.cloned.1.call-done = bf16[2048,256]{0,1:T(8,128)(2,1)} async-done(((bf16[2048,64]{0,1:T(8,128)(2,1)}), bf16[2048,256]{0,1:T(8,128)(2,1)}) %all-gather.4.cloned.1.call-update) | async-done | bytes 1048592 | tf_op jit(solution)/shard_map/all_gather | solution.py:19
  40.3 7.3 %fusion.10 = f32[2048,256]{0,1:T(8,128)} fusion(bf16[2048,2048]{1,0:T(8,128)(2,1)} %param.8, bf16[2048,256]{0,1:T(8,128)(2,1)} %all-gather.4.cloned.1.call-done), kind=kOutput, calls=%fused_computation.19 | convolution fusion | flops 2147483648 | bytes 11534336 | tf_op jit(solution)/shard_map/dot_general | solution.py:17
  47.6 0.0 reduce-scatter.5.cloned.1.call-update
  47.6 0.0 all-gather.6.cloned.1.call-start
  47.7 34.7 %reduce-scatter.5.cloned.1.call-done = f32[2048,64]{0,1:T(8,128)} async-done(((f32[2048,256]{0,1:T(8,128)}), f32[2048,64]{0,1:T(8,128)}) %reduce-scatter.5.cloned.1.call-update) | async-done | bytes 524304 | tf_op jit(solution)/shard_map/reduce_scatter | solution.py:22
  82.3 1.8 convert_element_type.53
  84.1 0.0 all-gather.6.cloned.1.call-update
  84.2 0.0 reduce-scatter.7.cloned.1.call-start
  84.2 27.1 %all-gather.6.cloned.1.call-done = bf16[2048,256]{0,1:T(8,128)(2,1)} async-done(((bf16[2048,64]{0,1:T(8,128)(2,1)}), bf16[2048,256]{0,1:T(8,128)(2,1)}) %all-gather.6.cloned.1.call-update) | async-done | bytes 1048592 | tf_op jit(solution)/shard_map/all_gather | solution.py:25
  111.3 2.7 convolution_bitcast_fusion
  114.0 0.0 reduce-scatter.7.cloned.1.call-update
  114.1 0.0 all-reduce.3.cloned.1.call-start
  114.1 0.2 subtract_reduce_fusion
  114.3 21.7 %reduce-scatter.7.cloned.1.call-done = f32[128,256]{0,1:T(8,128)} async-done(((f32[512,256]{0,1:T(8,128)}), f32[128,256]{0,1:T(8,128)}) %reduce-scatter.7.cloned.1.call-update) | async-done | bytes 131088 | tf_op jit(solution)/shard_map/reduce_scatter | solution.py:26
  136.0 0.9 convert_element_type.56
  136.9 1.9 all_gather.17
  138.9 0.1 copy.10
  139.0 0.4 fusion.5
  139.5 0.1 copy.11
  139.6 0.1 fusion.4
  139.7 4.8 %fusion = bf16[4096,256]{0,1:T(8,128)(2,1)} fusion(bf16[512,256]{1,0:T(8,128)(2,1)S(1)} %fusion.4, bf16[4096,512]{1,0:T(8,128)(2,1)} %param.10), kind=kOutput, calls=%fused_computation.1 | convolution fusion | flops 1074790400 | bytes 6553600 | tf_op jit(solution)/shard_map/dot_general | solution.py:40
  144.5 0.0 all-reduce.3.cloned.1.call-update
  144.5 0.0 all-reduce.5.cloned.1.call-start
  144.5 125.0 %all-reduce.3.cloned.1.call-done = bf16[4096,256]{0,1:T(8,128)(2,1)} async-done(((bf16[4096,256]{0,1:T(8,128)(2,1)}), bf16[4096,256]{0,1:T(8,128)(2,1)}) %all-reduce.3.cloned.1.call-update) | async-done | bytes 2097168 | tf_op jit(solution)/shard_map/psum | solution.py:41
  269.5 4.8 %fusion.3 = bf16[512,256]{0,1:T(8,128)(2,1)} fusion(bf16[4096,256]{0,1:T(8,128)(2,1)} %all-reduce.3.cloned.1.call-done, bf16[4096,512]{1,0:T(8,128)(2,1)} %param.10), kind=kOutput, calls=%fused_computation.8 | convolution fusion | flops 1073872896 | bytes 6553600 | tf_op jit(solution)/shard_map/dot_general | solution.py:8
  274.3 0.0 all-reduce.5.cloned.1.call-update
  274.3 0.0 reduce-scatter.9.cloned.1.call-start
  274.4 0.6 dynamic_slice.10
  275.6 16.3 %all-reduce.5.cloned.1.call-done = bf16[512,256]{0,1:T(8,128)(2,1)} async-done(((bf16[512,256]{0,1:T(8,128)(2,1)}), bf16[512,256]{0,1:T(8,128)(2,1)}) %all-reduce.5.cloned.1.call-update) | async-done | bytes 262160 | tf_op jit(solution)/shard_map/psum | solution.py:42
  291.9 0.8 constant_dynamic-slice_fusion
  292.8 13.1 %all_gather.18 = bf16[512,256]{0,1:T(8,128)(2,1)S(1)} all-gather(bf16[128,256]{0,1:T(8,128)(2,1)S(1)} %constant_dynamic-slice_fusion), channel_id=1, replica_groups=mesh['leaf'=2,'row'=4,'col'=4] {'col'}, dimensions={0}, use_global_device_ids=true | all-gather | bytes 327680 | tf_op jit(solution)/shard_map/all_gather | solution.py:49
  305.9 1.7 fusion.2
  307.6 0.0 reduce-scatter.9.cloned.1.call-update
  307.7 0.0 all-gather.8.cloned.1.call-start
  307.7 28.2 %reduce-scatter.9.cloned.1.call-done = bf16[2048,64]{0,1:T(8,128)(2,1)} async-done(((bf16[2048,256]{0,1:T(8,128)(2,1)}), bf16[2048,64]{0,1:T(8,128)(2,1)}) %reduce-scatter.9.cloned.1.call-update) | async-done | bytes 262160 | tf_op jit(solution)/shard_map/reduce_scatter | solution.py:52
  335.9 1.7 subtract_convert_fusion
  337.6 0.0 all-gather.8.cloned.1.call-update
  337.7 0.0 reduce-scatter.11.cloned.1.call-start
  337.7 27.2 %all-gather.8.cloned.1.call-done = bf16[2048,256]{0,1:T(8,128)(2,1)} async-done(((bf16[2048,64]{0,1:T(8,128)(2,1)}), bf16[2048,256]{0,1:T(8,128)(2,1)}) %all-gather.8.cloned.1.call-update) | async-done | bytes 1048592 | tf_op jit(solution)/shard_map/all_gather | solution.py:56
  364.9 7.0 %fusion.1 = bf16[2048,256]{0,1:T(8,128)(2,1)} fusion(bf16[2048,256]{0,1:T(8,128)(2,1)} %all-gather.8.cloned.1.call-done, bf16[2048,2048]{1,0:T(8,128)(2,1)} %param.8), kind=kOutput, calls=%fused_computation.4 | convolution fusion | flops 2148007936 | bytes 10485760 | tf_op jit(solution)/shard_map/dot_general | solution.py:8
  371.9 0.0 reduce-scatter.11.cloned.1.call-update
  371.9 0.9 copy.12
  372.9 26.5 %reduce-scatter.11.cloned.1.call-done = bf16[2048,64]{0,1:T(8,128)(2,1)} async-done(((bf16[2048,256]{0,1:T(8,128)(2,1)}), bf16[2048,64]{0,1:T(8,128)(2,1)}) %reduce-scatter.11.cloned.1.call-update) | async-done | bytes 262160 | tf_op jit(solution)/shard_map/reduce_scatter | solution.py:57
  399.4 1.8 convert_element_type.68
  (10 shorter events, 0.1 us)
Async XLA Ops:
  7.2 104.1 %copy-start = (bf16[2048,512]{1,0:T(8,128)(2,1)S(1)}, bf16[2048,512]{1,0:T(8,128)(2,1)}, u32[]{:S(2)}) copy-start(bf16[2048,512]{1,0:T(8,128)(2,1)} %param.9) | copy-start | bytes 6291460
  7.2 33.1 %all-gather.4.cloned.1.call-start = ((), (), s32[]{:S(2)}) async-start(), calls=%async_computation.4 | async-start | bytes 1310720 | tf_op jit(solution)/shard_map/all_gather | solution.py:19
  7.9 74.4 %reduce-scatter.5.cloned.1.call-start = ((), (), s32[]{:S(2)}) async-start(), calls=%async_computation.5 | async-start | bytes 2621440 | tf_op jit(solution)/shard_map/reduce_scatter | solution.py:22
  47.6 63.7 %all-gather.6.cloned.1.call-start = ((), (), s32[]{:S(2)}) async-start(), calls=%async_computation.6 | async-start | bytes 1310720 | tf_op jit(solution)/shard_map/all_gather | solution.py:25
  84.1 30.0 %copy-start.4 = (s32[2,16]{1,0:T(2,128)S(1)}, s32[2,16]{1,0:T(2,128)}, u32[]{:S(2)}) copy-start(s32[2,16]{1,0:T(2,128)} %param.11) | copy-start | bytes 388
  84.2 51.9 %reduce-scatter.7.cloned.1.call-start = ((), (), s32[]{:S(2)}) async-start(), calls=%async_computation.7 | async-start | bytes 655360 | tf_op jit(solution)/shard_map/reduce_scatter | solution.py:26
  114.0 25.5 %copy-start.3 = (bf16[512,256]{1,0:T(8,128)(2,1)S(1)}, bf16[512,256]{1,0:T(8,128)(2,1)}, u32[]{:S(2)}) copy-start(bf16[512,256]{1,0:T(8,128)(2,1)} %param.7) | copy-start | bytes 786436
  114.1 155.5 %all-reduce.3.cloned.1.call-start = ((), (), s32[]{:S(2)}) async-start(), calls=%async_computation.8 | async-start | bytes 4194304 | tf_op jit(solution)/shard_map/psum | solution.py:41
  144.5 147.4 %all-reduce.5.cloned.1.call-start = ((), (), s32[]{:S(2)}) async-start(), calls=%async_computation.9 | async-start | bytes 524288 | tf_op jit(solution)/shard_map/psum | solution.py:42
  274.3 61.6 %reduce-scatter.9.cloned.1.call-start = ((), (), s32[]{:S(2)}) async-start(), calls=%async_computation.10 | async-start | bytes 1310720 | tf_op jit(solution)/shard_map/reduce_scatter | solution.py:52
  305.9 30.0 %copy-start.1 = (f32[2048,64]{0,1:T(8,128)S(1)}, f32[2048,64]{0,1:T(8,128)}, u32[]{:S(2)}) copy-start(f32[2048,64]{0,1:T(8,128)} %reduce-scatter.5.cloned.1.call-done) | copy-start | bytes 1572868
  307.7 57.2 %all-gather.8.cloned.1.call-start = ((), (), s32[]{:S(2)}) async-start(), calls=%async_computation.11 | async-start | bytes 1310720 | tf_op jit(solution)/shard_map/all_gather | solution.py:56
  337.6 34.3 %copy-start.2 = (bf16[512,256]{0,1:T(8,128)(2,1)S(1)}, bf16[512,256]{0,1:T(8,128)(2,1)}, u32[]{:S(2)}) copy-start(bf16[512,256]{0,1:T(8,128)(2,1)} %all-reduce.5.cloned.1.call-done) | copy-start | bytes 786436
  337.7 61.7 %reduce-scatter.11.cloned.1.call-start = ((), (), s32[]{:S(2)}) async-start(), calls=%async_computation.12 | async-start | bytes 1310720 | tf_op jit(solution)/shard_map/reduce_scatter | solution.py:57
Sparse Core Ops, SparseCore 0:
  9.6 30.6 all-gather.3
  47.7 34.5 reduce-scatter.4
  84.8 26.4 all-gather.5
  114.2 21.8 reduce-scatter.6
  144.6 124.8 all-reduce.2
  274.4 17.4 all-reduce.4
  307.8 28.0 reduce-scatter.8
  338.3 26.4 all-gather.7
  372.0 27.2 reduce-scatter.10
where the time goes:
time: 408 us
  waiting for transfers between devices  340 us (83%)
  matrix products  28.8 us (7%)
  blocking collectives  15.1 us (4%)
  between operations  14.6 us (4%)
  other arithmetic  6.41 us (2%)
    psum x1, waiting for transfers between devices, shards(): sep_mid = lax.psum(sep_part.astype(jnp.bfloat16), ('row', 'col'))  125 us
    reduce_scatter x1, waiting for transfers between devices, shards(): lax.psum_scatter(partial_value, 'row', scatter_dimension=1, tiled=True)  34.7 us
    all_gather x1, waiting for transfers between devices, shards(): lax.all_gather(sketch_leaf, 'col', axis=1, tiled=True)  32.3 us
    reduce_scatter x1, waiting for transfers between devices, shards(): lax.psum_scatter(back_part.astype(jnp.bfloat16), 'row', scatter_dimension...  28.2 us
    all_gather x1, waiting for transfers between devices, shards(): lax.all_gather(leaf_rhs, 'row', axis=1, tiled=True)  27.2 us
    all_gather x1, waiting for transfers between devices, shards(): lax.all_gather(front_z, 'row', axis=1, tiled=True)  27.1 us
    reduce_scatter x1, waiting for transfers between devices, shards(): lax.psum_scatter(out_part.astype(jnp.bfloat16), 'col', scatter_dimension=...  26.5 us
    reduce_scatter x1, waiting for transfers between devices, shards(): lax.psum_scatter(coupled_part, 'col', scatter_dimension=0, tiled=True)  21.7 us
  transfers between devices with their start and end apart: 9, of which 9 were waited for; matrix products, arithmetic and copies ran while one was open for 0% of the time, Pallas kernels for 0%

commit v1 on v0

--- a/solution.py
+++ b/solution.py
@@ -38,7 +38,7 @@
     )
     sep_rhs = (sketch_sep.astype(jnp.float32) - total).astype(jnp.bfloat16)
     sep_part = jnp.dot(sep_inverse, sep_rhs, preferred_element_type=jnp.float32)
-    sep_mid = lax.psum(sep_part.astype(jnp.bfloat16), ("row", "col"))
+    sep_mid = lax.psum(lax.psum(sep_part.astype(jnp.bfloat16), "col"), "row")
     sketch_out_sep = lax.psum(
         contract_rows(sep_inverse, sep_mid).astype(jnp.bfloat16), "leaf"
     ).astype(jnp.float32)

time: 408 us -> 440 us (1.078)
  waiting for transfers between devices: 340 us -> 372 us
    psum x1 -> x2, waiting for transfers between devices: 125 us -> 156 us  [shards(): sep_mid = lax.psum(lax.psum(sep_part.astype(jnp.bfloat16), 'col'), 'row')]
  transfers between devices with their start and end apart: 9 -> 10, of which waited for: 9 -> 10; matrix products, arithmetic and copies ran while one was open for 0% -> 0% of each run, Pallas kernels for 0% -> 0%
where the time goes in v1:
time: 440 us
  waiting for transfers between devices  372 us (85%)
  matrix products  28.8 us (7%)
  blocking collectives  15.1 us (3%)
  between operations  14.9 us (3%)
  other arithmetic  6.41 us (1%)
    psum x2, waiting for transfers between devices, shards(): sep_mid = lax.psum(lax.psum(sep_part.astype(jnp.bfloat16), 'col'), 'row')  156 us
    reduce_scatter x1, waiting for transfers between devices, shards(): lax.psum_scatter(partial_value, 'row', scatter_dimension=1, tiled=True)  34.7 us
    all_gather x1, waiting for transfers between devices, shards(): lax.all_gather(sketch_leaf, 'col', axis=1, tiled=True)  32.3 us
    reduce_scatter x1, waiting for transfers between devices, shards(): lax.psum_scatter(back_part.astype(jnp.bfloat16), 'row', scatter_dimension...  28.2 us
    all_gather x1, waiting for transfers between devices, shards(): lax.all_gather(leaf_rhs, 'row', axis=1, tiled=True)  27.2 us
    all_gather x1, waiting for transfers between devices, shards(): lax.all_gather(front_z, 'row', axis=1, tiled=True)  27.1 us
    reduce_scatter x1, waiting for transfers between devices, shards(): lax.psum_scatter(out_part.astype(jnp.bfloat16), 'col', scatter_dimension=...  26.5 us
    reduce_scatter x1, waiting for transfers between devices, shards(): lax.psum_scatter(coupled_part, 'col', scatter_dimension=0, tiled=True)  21.7 us
  transfers between devices with their start and end apart: 10, of which 10 were waited for; matrix products, arithmetic and copies ran while one was open for 0% of the time, Pallas kernels for 0%

profile of v1, /device:TPU:0, one launch (start us, length us, event | category | flops | bytes accessed | tf_op | source)
XLA Modules:
  0.0 439.8 jit_solution(17107274212358703769)
XLA Ops:
  7.2 0.0 all-gather.4.cloned.1.call-start
  7.2 0.7 all-gather.4.cloned.1.call-update
  7.9 0.0 reduce-scatter.5.cloned.1.call-start
  8.0 32.3 %all-gather.4.cloned.1.call-done = bf16[2048,256]{0,1:T(8,128)(2,1)} async-done(((bf16[2048,64]{0,1:T(8,128)(2,1)}), bf16[2048,256]{0,1:T(8,128)(2,1)}) %all-gather.4.cloned.1.call-update) | async-done | bytes 1048592 | tf_op jit(solution)/shard_map/all_gather | solution.py:19
  40.3 7.3 %fusion.10 = f32[2048,256]{0,1:T(8,128)} fusion(bf16[2048,2048]{1,0:T(8,128)(2,1)} %param.8, bf16[2048,256]{0,1:T(8,128)(2,1)} %all-gather.4.cloned.1.call-done), kind=kOutput, calls=%fused_computation.19 | convolution fusion | flops 2147483648 | bytes 11534336 | tf_op jit(solution)/shard_map/dot_general | solution.py:17
  47.6 0.0 reduce-scatter.5.cloned.1.call-update
  47.6 0.0 all-gather.6.cloned.1.call-start
  47.7 34.7 %reduce-scatter.5.cloned.1.call-done = f32[2048,64]{0,1:T(8,128)} async-done(((f32[2048,256]{0,1:T(8,128)}), f32[2048,64]{0,1:T(8,128)}) %reduce-scatter.5.cloned.1.call-update) | async-done | bytes 524304 | tf_op jit(solution)/shard_map/reduce_scatter | solution.py:22
  82.3 1.8 convert_element_type.53
  84.1 0.0 all-gather.6.cloned.1.call-update
  84.2 0.0 reduce-scatter.7.cloned.1.call-start
  84.2 27.1 %all-gather.6.cloned.1.call-done = bf16[2048,256]{0,1:T(8,128)(2,1)} async-done(((bf16[2048,64]{0,1:T(8,128)(2,1)}), bf16[2048,256]{0,1:T(8,128)(2,1)}) %all-gather.6.cloned.1.call-update) | async-done | bytes 1048592 | tf_op jit(solution)/shard_map/all_gather | solution.py:25
  111.3 2.7 convolution_bitcast_fusion
  114.1 0.0 all-reduce.4.cloned.1.call-start
  114.1 0.2 subtract_reduce_fusion
  114.3 21.7 %reduce-scatter.7.cloned.1.call-done = f32[128,256]{0,1:T(8,128)} async-done(((f32[512,256]{0,1:T(8,128)}), f32[128,256]{0,1:T(8,128)}) %reduce-scatter.7.cloned.1.call-update) | async-done | bytes 131088 | tf_op jit(solution)/shard_map/reduce_scatter | solution.py:26
  136.0 0.9 convert_element_type.56
  136.9 1.9 all_gather.17
  138.9 0.1 copy.10
  139.0 0.4 fusion.5
  139.5 0.1 copy.11
  139.6 0.1 fusion.4
  139.7 4.8 %fusion = bf16[4096,256]{0,1:T(8,128)(2,1)} fusion(bf16[512,256]{1,0:T(8,128)(2,1)S(1)} %fusion.4, bf16[4096,512]{1,0:T(8,128)(2,1)} %param.10), kind=kOutput, calls=%fused_computation.1 | convolution fusion | flops 1074790400 | bytes 6553600 | tf_op jit(solution)/shard_map/dot_general | solution.py:40
  144.5 0.0 all-reduce.4.cloned.1.call-update
  144.5 0.0 all-reduce.6.cloned.1.call-start
  144.5 84.5 %all-reduce.4.cloned.1.call-done = bf16[4096,256]{0,1:T(8,128)(2,1)} async-done(((bf16[4096,256]{0,1:T(8,128)(2,1)}), bf16[4096,256]{0,1:T(8,128)(2,1)}) %all-reduce.4.cloned.1.call-update) | async-done | bytes 2097168 | tf_op jit(solution)/shard_map/psum | solution.py:41
  229.1 0.0 all-reduce.6.cloned.1.call-update
  229.1 0.0 all-reduce.8.cloned.1.call-start
  229.1 71.4 %all-reduce.6.cloned.1.call-done = bf16[4096,256]{0,1:T(8,128)(2,1)} async-done(((bf16[4096,256]{0,1:T(8,128)(2,1)}), bf16[4096,256]{0,1:T(8,128)(2,1)}) %all-reduce.6.cloned.1.call-update) | async-done | bytes 2097168 | tf_op jit(solution)/shard_map/psum | solution.py:41
  300.6 4.8 %fusion.3 = bf16[512,256]{0,1:T(8,128)(2,1)} fusion(bf16[4096,256]{0,1:T(8,128)(2,1)} %all-reduce.6.cloned.1.call-done, bf16[4096,512]{1,0:T(8,128)(2,1)} %param.10), kind=kOutput, calls=%fused_computation.8 | convolution fusion | flops 1073872896 | bytes 6553600 | tf_op jit(solution)/shard_map/dot_general | solution.py:8
  305.3 0.0 all-reduce.8.cloned.1.call-update
  305.4 0.0 reduce-scatter.9.cloned.1.call-start
  305.4 0.6 dynamic_slice.10
  306.7 17.1 %all-reduce.8.cloned.1.call-done = bf16[512,256]{0,1:T(8,128)(2,1)} async-done(((bf16[512,256]{0,1:T(8,128)(2,1)}), bf16[512,256]{0,1:T(8,128)(2,1)}) %all-reduce.8.cloned.1.call-update) | async-done | bytes 262160 | tf_op jit(solution)/shard_map/psum | solution.py:42
  323.8 0.8 constant_dynamic-slice_fusion
  324.6 13.1 %all_gather.18 = bf16[512,256]{0,1:T(8,128)(2,1)S(1)} all-gather(bf16[128,256]{0,1:T(8,128)(2,1)S(1)} %constant_dynamic-slice_fusion), channel_id=1, replica_groups=mesh['leaf'=2,'row'=4,'col'=4] {'col'}, dimensions={0}, use_global_device_ids=true | all-gather | bytes 327680 | tf_op jit(solution)/shard_map/all_gather | solution.py:49
  337.7 1.7 fusion.2
  339.5 0.0 reduce-scatter.9.cloned.1.call-update
  339.5 0.0 all-gather.8.cloned.1.call-start
  339.5 28.2 %reduce-scatter.9.cloned.1.call-done = bf16[2048,64]{0,1:T(8,128)(2,1)} async-done(((bf16[2048,256]{0,1:T(8,128)(2,1)}), bf16[2048,64]{0,1:T(8,128)(2,1)}) %reduce-scatter.9.cloned.1.call-update) | async-done | bytes 262160 | tf_op jit(solution)/shard_map/reduce_scatter | solution.py:52
  367.7 1.7 subtract_convert_fusion
  369.4 0.0 all-gather.8.cloned.1.call-update
  369.5 0.0 reduce-scatter.11.cloned.1.call-start
  369.5 27.2 %all-gather.8.cloned.1.call-done = bf16[2048,256]{0,1:T(8,128)(2,1)} async-done(((bf16[2048,64]{0,1:T(8,128)(2,1)}), bf16[2048,256]{0,1:T(8,128)(2,1)}) %all-gather.8.cloned.1.call-update) | async-done | bytes 1048592 | tf_op jit(solution)/shard_map/all_gather | solution.py:56
  396.7 7.0 %fusion.1 = bf16[2048,256]{0,1:T(8,128)(2,1)} fusion(bf16[2048,256]{0,1:T(8,128)(2,1)} %all-gather.8.cloned.1.call-done, bf16[2048,2048]{1,0:T(8,128)(2,1)} %param.8), kind=kOutput, calls=%fused_computation.4 | convolution fusion | flops 2148007936 | bytes 10485760 | tf_op jit(solution)/shard_map/dot_general | solution.py:8
  403.7 0.9 copy.12
  404.7 26.5 %reduce-scatter.11.cloned.1.call-done = bf16[2048,64]{0,1:T(8,128)(2,1)} async-done(((bf16[2048,256]{0,1:T(8,128)(2,1)}), bf16[2048,64]{0,1:T(8,128)(2,1)}) %reduce-scatter.11.cloned.1.call-update) | async-done | bytes 262160 | tf_op jit(solution)/shard_map/reduce_scatter | solution.py:57
  431.2 1.8 convert_element_type.68
  (13 shorter events, 0.1 us)
Async XLA Ops:
  7.2 104.1 %copy-start = (bf16[2048,512]{1,0:T(8,128)(2,1)S(1)}, bf16[2048,512]{1,0:T(8,128)(2,1)}, u32[]{:S(2)}) copy-start(bf16[2048,512]{1,0:T(8,128)(2,1)} %param.9) | copy-start | bytes 6291460
  7.2 33.1 %all-gather.4.cloned.1.call-start = ((), (), s32[]{:S(2)}) async-start(), calls=%async_computation.4 | async-start | bytes 1310720 | tf_op jit(solution)/shard_map/all_gather | solution.py:19
  7.9 74.4 %reduce-scatter.5.cloned.1.call-start = ((), (), s32[]{:S(2)}) async-start(), calls=%async_computation.5 | async-start | bytes 2621440 | tf_op jit(solution)/shard_map/reduce_scatter | solution.py:22
  47.6 63.7 %all-gather.6.cloned.1.call-start = ((), (), s32[]{:S(2)}) async-start(), calls=%async_computation.6 | async-start | bytes 1310720 | tf_op jit(solution)/shard_map/all_gather | solution.py:25
  84.1 30.0 %copy-start.4 = (s32[2,16]{1,0:T(2,128)S(1)}, s32[2,16]{1,0:T(2,128)}, u32[]{:S(2)}) copy-start(s32[2,16]{1,0:T(2,128)} %param.11) | copy-start | bytes 388
  84.2 51.9 %reduce-scatter.7.cloned.1.call-start = ((), (), s32[]{:S(2)}) async-start(), calls=%async_computation.7 | async-start | bytes 655360 | tf_op jit(solution)/shard_map/reduce_scatter | solution.py:26
  114.0 25.5 %copy-start.3 = (bf16[512,256]{1,0:T(8,128)(2,1)S(1)}, bf16[512,256]{1,0:T(8,128)(2,1)}, u32[]{:S(2)}) copy-start(bf16[512,256]{1,0:T(8,128)(2,1)} %param.7) | copy-start | bytes 786436
  114.1 115.0 %all-reduce.4.cloned.1.call-start = ((), (), s32[]{:S(2)}) async-start(), calls=%async_computation.8 | async-start | bytes 4194304 | tf_op jit(solution)/shard_map/psum | solution.py:41
  144.5 156.1 %all-reduce.6.cloned.1.call-start = ((), (), s32[]{:S(2)}) async-start(), calls=%async_computation.9 | async-start | bytes 4194304 | tf_op jit(solution)/shard_map/psum | solution.py:41
  229.1 94.7 %all-reduce.8.cloned.1.call-start = ((), (), s32[]{:S(2)}) async-start(), calls=%async_computation.10 | async-start | bytes 524288 | tf_op jit(solution)/shard_map/psum | solution.py:42
  305.4 62.4 %reduce-scatter.9.cloned.1.call-start = ((), (), s32[]{:S(2)}) async-start(), calls=%async_computation.11 | async-start | bytes 1310720 | tf_op jit(solution)/shard_map/reduce_scatter | solution.py:52
  337.7 30.0 %copy-start.1 = (f32[2048,64]{0,1:T(8,128)S(1)}, f32[2048,64]{0,1:T(8,128)}, u32[]{:S(2)}) copy-start(f32[2048,64]{0,1:T(8,128)} %reduce-scatter.5.cloned.1.call-done) | copy-start | bytes 1572868
  339.5 57.2 %all-gather.8.cloned.1.call-start = ((), (), s32[]{:S(2)}) async-start(), calls=%async_computation.12 | async-start | bytes 1310720 | tf_op jit(solution)/shard_map/all_gather | solution.py:56
  369.5 34.3 %copy-start.2 = (bf16[512,256]{0,1:T(8,128)(2,1)S(1)}, bf16[512,256]{0,1:T(8,128)(2,1)}, u32[]{:S(2)}) copy-start(bf16[512,256]{0,1:T(8,128)(2,1)} %all-reduce.8.cloned.1.call-done) | copy-start | bytes 786436
  369.5 61.7 %reduce-scatter.11.cloned.1.call-start = ((), (), s32[]{:S(2)}) async-start(), calls=%async_computation.13 | async-start | bytes 1310720 | tf_op jit(solution)/shard_map/reduce_scatter | solution.py:57
Sparse Core Ops, SparseCore 0:
  9.6 30.6 all-gather.3
  47.7 34.5 reduce-scatter.4
  84.8 26.4 all-gather.5
  114.2 21.8 reduce-scatter.6
  144.6 84.3 all-reduce.3
  232.0 68.5 all-reduce.5
  305.5 18.2 all-reduce.7
  339.6 28.0 reduce-scatter.8
  370.2 26.4 all-gather.7
  403.9 27.2 reduce-scatter.10
